TPU v7x, 32 devices: a whole 2x2x4 slice. The times are simulated.
32 devices in a mesh: tok: 4 (over y, x), row: 8 (over z, core).
Axes of the slice: x: 2, y: 2, z: 4, core: 2. Of those that a mesh axis runs over, the one named last changes fastest.
Arguments:
- hidden: bfloat16 [768, 28672], P('tok', 'row'), may hold values from -6 to 6
- resid: bfloat16 [768, 8192], P('tok', 'row'), may hold values from -6 to 6
- down_in: bfloat16 [28672, 256], P('row'), may hold values from -0.03125 to 0.03125
- down_out: bfloat16 [256, 8192], P(None, 'row'), may hold values from -0.375 to 0.375
- up_weight: bfloat16 [8192, 28672], P('row', 'tok'), may hold values from -0.0625 to 0.0625
- start: bfloat16 [28672, 256], P('tok'), may hold values from -6 to 6
Outputs:
- left_basis: float32 [8192, 256], P('row')
- right_basis: float32 [28672, 256], P(('tok', 'row'))
- core: float32 [256, 256], replicated
All inputs are finite; a program needn't handle non-finite values.
Results may differ from a plain program's by a relative error of at most 0.0004.
Values sent between devices are 32-bit elements; how exact they have to be, the bound alone decides.
A program may use at most 128 MiB of HBM per device.

v0:
```python
import math

import jax
import jax.numpy as jnp
from jax import lax
from jax.sharding import PartitionSpec as P

D = 8192
FW = 28672
ITERS = 2


HIGH = lax.Precision.HIGHEST


def inner(first, second):
    return lax.dot_general(
        first, second, (((0,), (0,)), ((), ())), precision=HIGH, preferred_element_type=jnp.float32
    )


def solve_lower(lower, block):
    return jax.scipy.linalg.solve_triangular(lower, block.T, lower=True).T


def shards(hidden, resid, down_in, down_out, up_weight, start):
    partial_value = jnp.dot(hidden, down_in, preferred_element_type=jnp.float32)
    code = lax.psum(partial_value, "row")
    act_full = resid.astype(jnp.float32) + jnp.dot(
        code, down_out.astype(jnp.float32), precision=HIGH
    )
    total_tokens = act_full.shape[0] * lax.axis_size("tok")

    def whiten(block):
        applied = lax.psum(jnp.dot(act_full, block, precision=HIGH), "row")
        return lax.psum(inner(act_full, applied), "tok") / total_tokens

    weight = up_weight.astype(jnp.float32)
    right = start.astype(jnp.float32)
    left = None
    back = None
    piece = None
    for step in range(ITERS):
        image = lax.psum(jnp.dot(weight, right, precision=HIGH), "tok")
        target = whiten(image)
        left_inner = lax.psum(inner(target, target), "row")
        lower = jnp.linalg.cholesky(left_inner)
        left = solve_lower(lower, target)
        back = whiten(left)
        share = lax.psum_scatter(inner(weight, back), "row", scatter_dimension=0, tiled=True)
        right_inner = lax.psum(inner(share, share), ("tok", "row"))
        right_lower = jnp.linalg.cholesky(right_inner)
        piece = solve_lower(right_lower, share)
        right = lax.all_gather(piece, "row", axis=0, tiled=True)
    core = lax.psum(inner(back, jnp.dot(weight, right, precision=HIGH)), ("tok", "row"))
    return (math.sqrt(D) * left, math.sqrt(FW) * piece, core)


def solution(mesh):
    placed = (
        P("tok", "row"),
        P("tok", "row"),
        P("row", None),
        P(None, "row"),
        P("row", "tok"),
        P("tok", None),
    )
    return jax.shard_map(
        shards,
        mesh=mesh,
        in_specs=placed,
        out_specs=(P("row", None), P(("tok", "row"), None), P()),
        check_vma=False,
    )
```

profile of v0, /device:TPU:0, one launch (start us, length us, event | category | flops | bytes accessed | tf_op | source)
XLA Modules:
  0.0 1771.4 jit_solution(3141381590307448974)
XLA Ops:
  8.7 2.5 fusion.69
  11.3 11.2 fusion.70
  22.6 46.1 %all-reduce.18.cloned.1.call-done = f32[192,256]{1,0:T(8,128)} async-done(((f32[192,256]{1,0:T(8,128)}), f32[192,256]{1,0:T(8,128)}) %all-reduce.18.cloned.1.call-update) | async-done | bytes 196624 | tf_op jit(solution)/shard_map/psum | solution.py:28
  70.1 54.1 %all-reduce.20.cloned.1.call-done = f32[1024,256]{1,0:T(8,128)} async-done(((f32[1024,256]{1,0:T(8,128)}), f32[1024,256]{1,0:T(8,128)}) %all-reduce.20.cloned.1.call-update) | async-done | bytes 1048592 | tf_op jit(solution)/shard_map/psum | solution.py:44
  124.2 2.7 fusion.71
  127.0 54.8 %all-reduce.22.cloned.1.call-done = f32[192,256]{1,0:T(8,128)} async-done(((f32[192,256]{1,0:T(8,128)}), f32[192,256]{1,0:T(8,128)}) %all-reduce.22.cloned.1.call-update) | async-done | bytes 196624 | tf_op jit(solution)/shard_map/psum | solution.py:35
  181.8 3.7 fusion.72
  185.6 51.6 %all-reduce.24.cloned.1.call-done = f32[1024,256]{1,0:T(8,128)} async-done(((f32[1024,256]{1,0:T(8,128)}), f32[1024,256]{1,0:T(8,128)}) %all-reduce.24.cloned.1.call-update) | async-done | bytes 1048592 | tf_op jit(solution)/shard_map/psum | solution.py:36
  237.2 4.1 fusion.10
  242.9 53.5 %all-reduce.26.cloned.1.call-done = f32[256,256]{0,1:T(8,128)} async-done(((f32[256,256]{0,1:T(8,128)}), f32[256,256]{0,1:T(8,128)}) %all-reduce.26.cloned.1.call-update) | async-done | bytes 262160 | tf_op jit(solution)/shard_map/psum | solution.py:46
  298.5 11.7 cholesky.214
  310.3 9.8 custom-call.19
  320.6 11.7 cholesky.231
  334.4 4.2 while.8
  338.6 19.7 %custom-call.20 = f32[2,128,128]{1,2,0:T(8,128)S(1)} custom-call(f32[2,128,128]{2,1,0:T(8,128)S(1)} %get-tuple-element.34), custom_call_target="InvertDiagBlocksLowerTriangular" | custom-call | tf_op jit(solution)/shard_map/jit(_solve_triangular)/triangular_solve | solution.py:23
  360.6 1.9 fusion
  362.5 53.7 %all-reduce.28.cloned.1.call-done = f32[192,256]{1,0:T(8,128)} async-done(((f32[192,256]{1,0:T(8,128)}), f32[192,256]{1,0:T(8,128)}) %all-reduce.28.cloned.1.call-update) | async-done | bytes 196624 | tf_op jit(solution)/shard_map/psum | solution.py:35
  416.2 3.7 fusion.73
  420.0 51.6 %all-reduce.30.cloned.1.call-done = f32[1024,256]{1,0:T(8,128)} async-done(((f32[1024,256]{1,0:T(8,128)}), f32[1024,256]{1,0:T(8,128)}) %all-reduce.30.cloned.1.call-update) | async-done | bytes 1048592 | tf_op jit(solution)/shard_map/psum | solution.py:36
  471.7 17.2 convolution_bitcast_fusion.1
  489.0 79.8 %reduce-scatter.3.cloned.1.call-done = f32[896,256]{0,1:T(8,128)} async-done(((f32[7168,256]{0,1:T(8,128)}), f32[896,256]{0,1:T(8,128)}) %reduce-scatter.3.cloned.1.call-update) | async-done | bytes 917520 | tf_op jit(solution)/shard_map/reduce_scatter | solution.py:50
  568.8 3.3 fusion.74
  572.6 125.7 %all-reduce.32.cloned.1.call-done = f32[256,256]{0,1:T(8,128)} async-done(((f32[256,256]{0,1:T(8,128)}), f32[256,256]{0,1:T(8,128)}) %all-reduce.32.cloned.1.call-update) | async-done | bytes 262160 | tf_op jit(solution)/shard_map/psum | solution.py:51
  700.4 11.7 cholesky.248
  712.8 9.8 custom-call.21
  723.1 11.7 cholesky.265
  736.9 4.2 while.9
  741.0 19.7 %custom-call.22 = f32[2,128,128]{1,2,0:T(8,128)S(1)} custom-call(f32[2,128,128]{2,1,0:T(8,128)S(1)} %get-tuple-element.35), custom_call_target="InvertDiagBlocksLowerTriangular" | custom-call | tf_op jit(solution)/shard_map/jit(_solve_triangular)/triangular_solve | solution.py:23
  760.7 1.6 fusion.24
  764.5 72.5 %all-gather.3.cloned.1.call-done = f32[7168,256]{0,1:T(8,128)} async-done(((f32[896,256]{0,1:T(8,128)}), f32[7168,256]{0,1:T(8,128)}) %all-gather.3.cloned.1.call-update) | async-done | bytes 7340048 | tf_op jit(solution)/shard_map/all_gather | solution.py:54
  837.0 16.9 convolution_bitcast_fusion.2
  854.0 51.3 %all-reduce.34.cloned.1.call-done = f32[1024,256]{0,1:T(8,128)} async-done(((f32[1024,256]{0,1:T(8,128)}), f32[1024,256]{0,1:T(8,128)}) %all-reduce.34.cloned.1.call-update) | async-done | bytes 1048592 | tf_op jit(solution)/shard_map/psum | solution.py:44
  905.3 3.1 fusion.75
  908.7 54.5 %all-reduce.36.cloned.1.call-done = f32[192,256]{1,0:T(8,128)} async-done(((f32[192,256]{1,0:T(8,128)}), f32[192,256]{1,0:T(8,128)}) %all-reduce.36.cloned.1.call-update) | async-done | bytes 196624 | tf_op jit(solution)/shard_map/psum | solution.py:35
  963.2 3.7 fusion.76
  967.0 51.7 %all-reduce.38.cloned.1.call-done = f32[1024,256]{1,0:T(8,128)} async-done(((f32[1024,256]{1,0:T(8,128)}), f32[1024,256]{1,0:T(8,128)}) %all-reduce.38.cloned.1.call-update) | async-done | bytes 1048592 | tf_op jit(solution)/shard_map/psum | solution.py:36
  1018.7 4.1 fusion.8
  1024.1 53.7 %all-reduce.40.cloned.1.call-done = f32[256,256]{0,1:T(8,128)} async-done(((f32[256,256]{0,1:T(8,128)}), f32[256,256]{0,1:T(8,128)}) %all-reduce.40.cloned.1.call-update) | async-done | bytes 262160 | tf_op jit(solution)/shard_map/psum | solution.py:46
  1079.9 11.7 cholesky.282
  1092.3 9.8 custom-call.23
  1102.6 11.7 cholesky.299
  1116.4 4.4 while.10
  1120.8 19.7 %custom-call.24 = f32[2,128,128]{1,2,0:T(8,128)S(1)} custom-call(f32[2,128,128]{2,1,0:T(8,128)S(1)} %get-tuple-element.36), custom_call_target="InvertDiagBlocksLowerTriangular" | custom-call | tf_op jit(solution)/shard_map/jit(_solve_triangular)/triangular_solve | solution.py:23
  1142.8 1.9 fusion.12
  1144.7 53.7 %all-reduce.42.cloned.1.call-done = f32[192,256]{1,0:T(8,128)} async-done(((f32[192,256]{1,0:T(8,128)}), f32[192,256]{1,0:T(8,128)}) %all-reduce.42.cloned.1.call-update) | async-done | bytes 196624 | tf_op jit(solution)/shard_map/psum | solution.py:35
  1198.4 3.7 fusion.77
  1202.2 51.6 %all-reduce.44.cloned.1.call-done = f32[1024,256]{1,0:T(8,128)} async-done(((f32[1024,256]{1,0:T(8,128)}), f32[1024,256]{1,0:T(8,128)}) %all-reduce.44.cloned.1.call-update) | async-done | bytes 1048592 | tf_op jit(solution)/shard_map/psum | solution.py:36
  1253.9 17.2 convolution_bitcast_fusion
  1271.1 79.8 %reduce-scatter.5.cloned.1.call-done = f32[896,256]{0,1:T(8,128)} async-done(((f32[7168,256]{0,1:T(8,128)}), f32[896,256]{0,1:T(8,128)}) %reduce-scatter.5.cloned.1.call-update) | async-done | bytes 917520 | tf_op jit(solution)/shard_map/reduce_scatter | solution.py:50
  1350.9 3.4 fusion.78
  1354.7 126.6 %all-reduce.46.cloned.1.call-done = f32[256,256]{0,1:T(8,128)} async-done(((f32[256,256]{0,1:T(8,128)}), f32[256,256]{0,1:T(8,128)}) %all-reduce.46.cloned.1.call-update) | async-done | bytes 262160 | tf_op jit(solution)/shard_map/psum | solution.py:51
  1483.3 11.7 cholesky.316
  1495.7 9.8 custom-call.25
  1506.0 11.7 cholesky.333
  1519.8 4.3 while.11
  1524.0 19.7 %custom-call.26 = f32[2,128,128]{1,2,0:T(8,128)S(1)} custom-call(f32[2,128,128]{2,1,0:T(8,128)S(1)} %get-tuple-element.37), custom_call_target="InvertDiagBlocksLowerTriangular" | custom-call | tf_op jit(solution)/shard_map/jit(_solve_triangular)/triangular_solve | solution.py:23
  1543.7 1.6 fusion.22
  1548.7 2.5 copy.17
  1551.2 68.8 %all-gather.5.cloned.1.call-done = f32[7168,256]{0,1:T(8,128)} async-done(((f32[896,256]{0,1:T(8,128)}), f32[7168,256]{0,1:T(8,128)}) %all-gather.5.cloned.1.call-update) | async-done | bytes 7340048 | tf_op jit(solution)/shard_map/all_gather | solution.py:54
  1620.0 16.1 fusion.79
  1636.1 2.6 fusion.5
  1639.7 2.4 copy.18
  1642.1 120.3 %all-reduce.48.cloned.1.call-done = f32[256,256]{1,0:T(8,128)} async-done(((f32[256,256]{1,0:T(8,128)}), f32[256,256]{1,0:T(8,128)}) %all-reduce.48.cloned.1.call-update) | async-done | bytes 262160 | tf_op jit(solution)/shard_map/psum | solution.py:55
  1762.5 1.7 copy.81
  (144 shorter events, 49.7 us)
Async XLA Ops:
  7.2 1.5 copy-start
  7.2 61.5 %all-reduce.18.cloned.1.call-start = ((), (), s32[]{:S(2)}) async-start(), calls=%async_computation.2 | async-start | bytes 393216 | tf_op jit(solution)/shard_map/psum | solution.py:28
  11.2 57.4 %copy-start.5 = (bf16[256,1024]{1,0:T(8,128)(2,1)S(1)}, bf16[256,1024]{1,0:T(8,128)(2,1)}, u32[]{:S(2)}) copy-start(bf16[256,1024]{1,0:T(8,128)(2,1)} %param.14) | copy-start | bytes 1572868
  11.3 57.4 %copy-start.6 = (bf16[192,1024]{1,0:T(8,128)(2,1)S(1)}, bf16[192,1024]{1,0:T(8,128)(2,1)}, u32[]{:S(2)}) copy-start(bf16[192,1024]{1,0:T(8,128)(2,1)} %param.12) | copy-start | bytes 1179652
  11.3 112.9 %all-reduce.20.cloned.1.call-start = ((), (), s32[]{:S(2)}) async-start(), calls=%async_computation.3 | async-start | bytes 2097152 | tf_op jit(solution)/shard_map/psum | solution.py:44
  22.5 159.2 %all-reduce.22.cloned.1.call-start = ((), (), s32[]{:S(2)}) async-start(), calls=%async_computation.4 | async-start | bytes 393216 | tf_op jit(solution)/shard_map/psum | solution.py:35
  126.9 110.3 %all-reduce.24.cloned.1.call-start = ((), (), s32[]{:S(2)}) async-start(), calls=%async_computation.5 | async-start | bytes 2097152 | tf_op jit(solution)/shard_map/psum | solution.py:36
  185.5 110.9 %all-reduce.26.cloned.1.call-start = ((), (), s32[]{:S(2)}) async-start(), calls=%async_computation.6 | async-start | bytes 524288 | tf_op jit(solution)/shard_map/psum | solution.py:46
  241.3 174.9 %all-reduce.28.cloned.1.call-start = ((), (), s32[]{:S(2)}) async-start(), calls=%async_computation.7 | async-start | bytes 393216 | tf_op jit(solution)/shard_map/psum | solution.py:35
  362.5 109.2 %all-reduce.30.cloned.1.call-start = ((), (), s32[]{:S(2)}) async-start(), calls=%async_computation.8 | async-start | bytes 2097152 | tf_op jit(solution)/shard_map/psum | solution.py:36
  420.0 148.8 %reduce-scatter.3.cloned.1.call-start = ((), (), s32[]{:S(2)}) async-start(), calls=%async_computation.9 | async-start | bytes 8257536 | tf_op jit(solution)/shard_map/reduce_scatter | solution.py:50
  488.9 209.4 %all-reduce.32.cloned.1.call-start = ((), (), s32[]{:S(2)}) async-start(), calls=%async_computation.10 | async-start | bytes 524288 | tf_op jit(solution)/shard_map/psum | solution.py:51
  568.8 193.5 %copy-start.3 = (f32[896,256]{0,1:T(8,128)S(1)}, f32[896,256]{0,1:T(8,128)}, u32[]{:S(2)}) copy-start(f32[896,256]{0,1:T(8,128)} %reduce-scatter.3.cloned.1.call-done) | copy-start | bytes 2752516
  572.1 264.9 %all-gather.3.cloned.1.call-start = ((), (), s32[]{:S(2)}) async-start(), calls=%async_computation.11 | async-start | bytes 8257536 | tf_op jit(solution)/shard_map/all_gather | solution.py:54
  764.4 140.8 %all-reduce.34.cloned.1.call-start = ((), (), s32[]{:S(2)}) async-start(), calls=%async_computation.12 | async-start | bytes 2097152 | tf_op jit(solution)/shard_map/psum | solution.py:44
  854.0 109.2 %all-reduce.36.cloned.1.call-start = ((), (), s32[]{:S(2)}) async-start(), calls=%async_computation.13 | async-start | bytes 393216 | tf_op jit(solution)/shard_map/psum | solution.py:35
  908.4 110.3 %all-reduce.38.cloned.1.call-start = ((), (), s32[]{:S(2)}) async-start(), calls=%async_computation.14 | async-start | bytes 2097152 | tf_op jit(solution)/shard_map/psum | solution.py:36
  966.9 110.9 %all-reduce.40.cloned.1.call-start = ((), (), s32[]{:S(2)}) async-start(), calls=%async_computation.15 | async-start | bytes 524288 | tf_op jit(solution)/shard_map/psum | solution.py:46
  1022.8 175.7 %all-reduce.42.cloned.1.call-start = ((), (), s32[]{:S(2)}) async-start(), calls=%async_computation.16 | async-start | bytes 393216 | tf_op jit(solution)/shard_map/psum | solution.py:35
  1144.7 109.2 %all-reduce.44.cloned.1.call-start = ((), (), s32[]{:S(2)}) async-start(), calls=%async_computation.17 | async-start | bytes 2097152 | tf_op jit(solution)/shard_map/psum | solution.py:36
  1202.2 148.7 %reduce-scatter.5.cloned.1.call-start = ((), (), s32[]{:S(2)}) async-start(), calls=%async_computation.18 | async-start | bytes 8257536 | tf_op jit(solution)/shard_map/reduce_scatter | solution.py:50
  1271.1 210.1 %all-reduce.46.cloned.1.call-start = ((), (), s32[]{:S(2)}) async-start(), calls=%async_computation.19 | async-start | bytes 524288 | tf_op jit(solution)/shard_map/psum | solution.py:51
  1350.9 194.4 %copy-start.2 = (f32[896,256]{0,1:T(8,128)S(1)}, f32[896,256]{0,1:T(8,128)}, u32[]{:S(2)}) copy-start(f32[896,256]{0,1:T(8,128)} %reduce-scatter.5.cloned.1.call-done) | copy-start | bytes 2752516
  1354.4 265.6 %all-gather.5.cloned.1.call-start = ((), (), s32[]{:S(2)}) async-start(), calls=%async_computation.20 | async-start | bytes 8257536 | tf_op jit(solution)/shard_map/all_gather | solution.py:54
  1547.4 215.1 %all-reduce.48.cloned.1.call-start = ((), (), s32[]{:S(2)}) async-start(), calls=%async_computation.21 | async-start | bytes 524288 | tf_op jit(solution)/shard_map/psum | solution.py:55
  1620.0 16.1 copy-start.4
  1620.0 144.2 %copy-start.1 = (bf16[3584,256]{1,0:T(8,128)(2,1)S(1)}, bf16[3584,256]{1,0:T(8,128)(2,1)}, u32[]{:S(2)}) copy-start(bf16[3584,256]{1,0:T(8,128)(2,1)} %param.13) | copy-start | bytes 5505028
Sparse Core Ops, SparseCore 0:
  11.4 57.2 all-reduce.17
  72.6 51.5 all-reduce.19
  127.2 54.5 all-reduce.21
  185.7 51.5 all-reduce.23
  241.5 54.9 all-reduce.25
  362.6 53.5 all-reduce.27
  420.1 51.5 all-reduce.29
  489.1 79.6 reduce-scatter.2
  574.9 123.3 all-reduce.31
  764.6 72.3 all-gather.2
  854.1 51.1 all-reduce.33
  908.5 54.6 all-reduce.35
  967.1 51.5 all-reduce.37
  1022.9 54.9 all-reduce.39
  1144.8 53.5 all-reduce.41
  1202.3 51.5 all-reduce.43
  1271.2 79.6 reduce-scatter.4
  1357.8 123.3 all-reduce.45
  1547.5 72.3 all-gather.4
  1638.8 123.5 all-reduce.47
where the time goes:
time: 1780 us; the launch traced here: 1770 us
  waiting for transfers between devices  1360 us (76%)
  other arithmetic  227 us (13%)
  matrix products  136 us (8%)
  local copies, waits for them, and re-layouts  28.4 us (2%)
  between operations  20.5 us (1%)
    psum x2, waiting for transfers between devices, shards(): right_inner = lax.psum(inner(share, share), ('tok', 'row'))  252 us
    psum x4, waiting for transfers between devices, whiten(): applied = lax.psum(jnp.dot(act_full, block, precision=HIGH), 'row')  217 us
    psum x4, waiting for transfers between devices, whiten(): return lax.psum(inner(act_full, applied), 'tok') / total_tokens  207 us
    reduce_scatter x2, waiting for transfers between devices, shards(): lax.psum_scatter(inner(weight, back), 'row', scatter_dimension=0, tiled=T...  160 us
    all_gather x2, waiting for transfers between devices, shards(): right = lax.all_gather(piece, 'row', axis=0, tiled=True)  141 us
    psum x1, waiting for transfers between devices, shards(): lax.psum(inner(back, jnp.dot(weight, right, precision=HIGH)), ('tok', 'ro...  120 us
    psum x2, waiting for transfers between devices, shards(): left_inner = lax.psum(inner(target, target), 'row')  107 us
    psum x2, waiting for transfers between devices, shards(): image = lax.psum(jnp.dot(weight, right, precision=HIGH), 'tok')  105 us
  transfers between devices with their start and end apart: 20, of which 20 were waited for; matrix products, arithmetic and copies ran while one was open for 1% of the time, Pallas kernels for 0%

commit v1 on v0

v1 whole, which is shorter than its diff:
```python
import math

import jax
import jax.numpy as jnp
from jax import lax
from jax.experimental import pallas as pl
from jax.experimental.pallas import tpu as pltpu
from jax.sharding import PartitionSpec as P

ITERS = 2
HIGH = lax.Precision.HIGHEST
F32 = jnp.float32
BF16 = jnp.bfloat16


def inner(first, second):
    return lax.dot_general(
        first, second, (((0,), (0,)), ((), ())), precision=HIGH, preferred_element_type=F32
    )


def outer(first, second):
    return lax.dot_general(
        first, second, (((1,), (1,)), ((), ())), precision=HIGH, preferred_element_type=F32
    )


def solve_lower(lower, block):
    return jax.scipy.linalg.solve_triangular(lower, block.T, lower=True).T


def activations(hidden, resid, down_in, down_out):
    partial_value = jnp.dot(hidden, down_in, preferred_element_type=F32)
    code = lax.psum(partial_value, "row")
    return resid.astype(F32) + jnp.dot(code, down_out.astype(F32), precision=HIGH)


def feature_space(hidden, resid, down_in, down_out, up_weight, start):
    act_full = activations(hidden, resid, down_in, down_out)
    total_tokens = act_full.shape[0] * lax.axis_size("tok")
    features = up_weight.shape[0] * lax.axis_size("row")
    columns = up_weight.shape[1] * lax.axis_size("tok")

    def whiten(block):
        applied = lax.psum(jnp.dot(act_full, block, precision=HIGH), "row")
        return lax.psum(inner(act_full, applied), "tok") / total_tokens

    weight = up_weight.astype(F32)
    right = start.astype(F32)
    for step in range(ITERS):
        image = lax.psum(jnp.dot(weight, right, precision=HIGH), "tok")
        target = whiten(image)
        lower = jnp.linalg.cholesky(lax.psum(inner(target, target), "row"))
        left = solve_lower(lower, target)
        back = whiten(left)
        share = lax.psum_scatter(inner(weight, back), "row", scatter_dimension=0, tiled=True)
        right_lower = jnp.linalg.cholesky(lax.psum(inner(share, share), ("tok", "row")))
        piece = solve_lower(right_lower, share)
        right = lax.all_gather(piece, "row", axis=0, tiled=True)
    core = lax.psum(inner(back, jnp.dot(weight, right, precision=HIGH)), ("tok", "row"))
    return (math.sqrt(features) * left, math.sqrt(columns) * piece, core)


def split_rows(block):
    first = lax.reduce_precision(block, 8, 7)
    rest = block - first
    second = lax.reduce_precision(rest, 8, 7)
    third = rest - second
    return first.astype(BF16), second.astype(BF16), third.astype(BF16)


def product_kernel(first_ref, second_ref, third_ref, weight_ref, out_ref):
    weight = weight_ref[...]
    total = jnp.dot(third_ref[...], weight, preferred_element_type=F32)
    total += jnp.dot(second_ref[...], weight, preferred_element_type=F32)
    total += jnp.dot(first_ref[...], weight, preferred_element_type=F32)
    out_ref[0] = total


def applied_blocks(parts, weight, blocks):
    tokens, depth = parts[0].shape
    width = weight.shape[1] // blocks
    whole = pl.BlockSpec((tokens, depth), lambda i: (0, 0))
    return pl.pallas_call(
        product_kernel,
        grid=(blocks,),
        in_specs=[whole, whole, whole, pl.BlockSpec((depth, width), lambda i: (0, i))],
        out_specs=pl.BlockSpec((1, tokens, width), lambda i: (i, 0, 0)),
        out_shape=jax.ShapeDtypeStruct((blocks, tokens, width), F32),
        compiler_params=pltpu.CompilerParams(vmem_limit_bytes=48 * 2**20),
        cost_estimate=pl.CostEstimate(
            flops=6 * tokens * depth * weight.shape[1],
            bytes_accessed=4 * tokens * weight.shape[1] + 2 * weight.size,
            transcendentals=0,
        ),
    )(*parts, weight)


def inverse_factor(table):
    size = table.shape[0]
    nb = 64
    eye = (
        lax.broadcasted_iota(jnp.int32, (nb, nb), 0) == lax.broadcasted_iota(jnp.int32, (nb, nb), 1)
    ).astype(F32)
    index = lax.broadcasted_iota(jnp.int32, (nb, 1), 0)
    for at in range(0, size, nb):
        work = jnp.concatenate([table[at : at + nb, at : at + nb], eye], axis=1)
        for j in range(nb):
            scale = lax.rsqrt(work[j : j + 1, j : j + 1])
            row = work[j : j + 1, :] * scale
            column = work[:, j : j + 1] * scale
            work = jnp.where(index == j, row, work - jnp.where(index < j, 0.0, column) * row)
        small = work[:, nb:]
        rows = jnp.dot(small, table[at : at + nb, :], precision=HIGH, preferred_element_type=F32)
        table[at : at + nb, :] = rows
        if at + nb < size:
            below = rows[:, at + nb : size]
            table[at + nb :, :] = table[at + nb :, :] - inner(below, rows)


def coefficient_kernel(gram_ref, square_ref, imaged_ref, left_ref, right_ref, core_ref, grams, now, table):
    tokens, size = imaged_ref.shape
    pltpu.sync_copy(gram_ref, grams.at[0])
    pltpu.sync_copy(square_ref, grams.at[1])
    now[...] = imaged_ref[...] / tokens
    eye = (
        lax.broadcasted_iota(jnp.int32, (size, size), 0)
        == lax.broadcasted_iota(jnp.int32, (size, size), 1)
    ).astype(F32)

    def one(i, carry):
        block = now[...]
        mapped = jnp.dot(grams[lax.rem(i, 2)], block, precision=HIGH, preferred_element_type=F32)
        table[:, :size] = inner(block, mapped)
        table[:, size:] = eye
        inverse_factor(table)
        inverse = table[:, size:]
        left_ref[...] = right_ref[...]
        right_ref[...] = outer(block, inverse)
        turned = outer(mapped, inverse)
        core_ref[...] = inner(block, turned)
        now[...] = turned / tokens
        return carry

    right_ref[...] = jnp.zeros_like(right_ref)
    lax.fori_loop(0, 2 * ITERS, one, 0)


def coefficients(gram, square, imaged):
    tokens, size = imaged.shape
    tall = jax.ShapeDtypeStruct((tokens, size), F32)
    vmem = pl.BlockSpec(memory_space=pltpu.VMEM)
    return pl.pallas_call(
        coefficient_kernel,
        in_specs=[pl.BlockSpec(memory_space=pl.ANY)] * 2 + [vmem],
        out_specs=[vmem] * 3,
        out_shape=[tall, tall, jax.ShapeDtypeStruct((size, size), F32)],
        scratch_shapes=[
            pltpu.VMEM((2, tokens, tokens), F32),
            pltpu.VMEM((tokens, size), F32),
            pltpu.VMEM((size, 2 * size), F32),
        ],
        compiler_params=pltpu.CompilerParams(vmem_limit_bytes=48 * 2**20),
    )(gram, square, imaged)


def token_space(hidden, resid, down_in, down_out, up_weight, start):
    blocks = lax.axis_size("row")
    tokens = hidden.shape[0] * lax.axis_size("tok")
    features = up_weight.shape[0] * blocks
    columns = up_weight.shape[1] * lax.axis_size("tok")
    width = up_weight.shape[1] // blocks
    own = lax.axis_index("row")

    code = lax.psum(jnp.dot(hidden, down_in, preferred_element_type=F32), "row")
    code = lax.all_gather(code, "tok", axis=0, tiled=True)
    base = lax.all_gather(resid.astype(F32), "tok", axis=0, tiled=True)
    acts = base + jnp.dot(code, down_out.astype(F32), precision=HIGH)
    gram = lax.psum(outer(acts, acts), "row")

    parts = split_rows(acts)
    chunk = 256 if tokens % 256 == 0 else tokens
    pieces = []
    for at in range(0, tokens, chunk):
        block = applied_blocks([p[at : at + chunk] for p in parts], up_weight, blocks)
        pieces.append(lax.psum_scatter(block, "row", scatter_dimension=0, tiled=True)[0])
    applied = jnp.concatenate(pieces, axis=0)

    begin = lax.dynamic_slice_in_dim(start, own * width, width, axis=0).astype(F32)
    sums = jnp.concatenate(
        [outer(applied, applied), jnp.dot(applied, begin, precision=HIGH)], axis=1
    )
    sums = lax.psum(sums, ("tok", "row"))
    square, imaged = sums[:, :tokens], sums[:, tokens:]

    left_coef, right_coef, core = coefficients(gram, square, imaged)
    left = inner(acts, left_coef)
    right = inner(applied, right_coef)
    return (math.sqrt(features) * left, math.sqrt(columns) * right, core)


def shards(hidden, *rest):
    tokens = hidden.shape[0] * lax.axis_size("tok")
    if tokens > 1024:
        return feature_space(hidden, *rest)
    return token_space(hidden, *rest)


def solution(mesh):
    placed = (
        P("tok", "row"),
        P("tok", "row"),
        P("row", None),
        P(None, "row"),
        P("row", "tok"),
        P("tok", None),
    )
    return jax.shard_map(
        shards,
        mesh=mesh,
        in_specs=placed,
        out_specs=(P("row", None), P(("tok", "row"), None), P()),
        check_vma=False,
    )
```

time: 1780 us -> 722 us (0.41)
  waiting for transfers between devices: 1360 us -> 449 us
  other arithmetic: 227 us -> 3.07 us
  Pallas kernels: 0 us -> 183 us
  matrix products: 136 us -> 41.6 us
  local copies, waits for them, and re-layouts: 28.4 us -> 9.68 us
    psum x16 -> x3, waiting for transfers between devices: 1050 us -> 245 us  [the longest x1 125 us: token_space(): sums = lax.psum(sums, ('tok', 'row'))]
    another operation x36 -> x0, other arithmetic: 217 us -> none  [the longest x9 78.8 us: solve_lower(): return jax.scipy.linalg.solve_triangular(lower, block.T, lower=True).T]
    pallas_call x0 -> x4, Pallas kernels: none -> 183 us  [the longest x1 131 us: coefficients(): pl.pallas_call(coefficient_kernel, in_specs=[pl.BlockSpec(memory_space=pl...]
    all_gather x2 -> x1, waiting for transfers between devices: 141 us -> 0.01 us  [token_space(): base = lax.all_gather(resid.astype(F32), 'tok', axis=0, tiled=True)]
    dot_general x11 -> x2, matrix products: 66.8 us -> 11.4 us  [inner(): lax.dot_general(first, second, (((0,), (0,)), ((), ())), precision=HIGH,...]
    reduce_scatter x2 -> x3, waiting for transfers between devices: 160 us -> 204 us  [token_space(): lax.psum_scatter(block, 'row', scatter_dimension=0, tiled=True)[0]]
    dot_general x9 -> x5, matrix products: 57.8 us -> 30.2 us  [the longest x2 19.6 us: outer(): lax.dot_general(first, second, (((1,), (1,)), ((), ())), precision=HIGH,...]
  transfers between devices with their start and end apart: 20 -> 7, of which waited for: 20 -> 6; matrix products, arithmetic and copies ran while one was open for 1% -> 2% of each run, Pallas kernels for 0% -> 5%
where the time goes in v1:
time: 722 us; the launch traced here: 715 us
  waiting for transfers between devices  449 us (62%)
  Pallas kernels  183 us (25%)
  matrix products  41.6 us (6%)
  between operations  15.8 us (2%)
  blocking collectives  12.4 us (2%)
  local copies, waits for them, and re-layouts  9.68 us (1%)
    reduce_scatter x3, waiting for transfers between devices, token_space(): lax.psum_scatter(block, 'row', scatter_dimension=0, tiled=True)[0]  204 us
    pallas_call x1, Pallas kernels, coefficients(): pl.pallas_call(coefficient_kernel, in_specs=[pl.BlockSpec(memory_space=pl...  131 us
    psum x1, waiting for transfers between devices, token_space(): sums = lax.psum(sums, ('tok', 'row'))  125 us
    psum x1, waiting for transfers between devices, token_space(): gram = lax.psum(outer(acts, acts), 'row')  63.7 us
    psum x1, waiting for transfers between devices, token_space(): code = lax.psum(jnp.dot(hidden, down_in, preferred_element_type=F32), 'row')  56.3 us
    pallas_call x3, Pallas kernels, applied_blocks(): pl.pallas_call(product_kernel, grid=(blocks,), in_specs=[whole, whole, wh...  51.4 us
    dot_general x2, matrix products, outer(): lax.dot_general(first, second, (((1,), (1,)), ((), ())), precision=HIGH,...  19.6 us
  transfers between devices with their start and end apart: 7, of which 6 were waited for; matrix products, arithmetic and copies ran while one was open for 2% of the time, Pallas kernels for 5%

profile of v1, /device:TPU:0, one launch (start us, length us, event | category | flops | bytes accessed | tf_op | source)
XLA Modules:
  0.0 714.7 jit_solution(15308667455355757594)
XLA Ops:
  8.0 0.0 copy-start
  8.0 0.0 copy-start.6
  8.0 0.0 copy-start.5
  8.0 0.0 all-reduce.4.cloned.1.call-start
  8.1 1.4 copy-done
  9.5 2.5 fusion.11
  12.0 0.0 all-reduce.4.cloned.1.call-update
  12.1 0.0 all-gather.2.cloned.1.call-start
  12.1 0.0 copy-done.6
  12.1 1.0 convert_element_type.14
  13.1 0.0 all-gather.2.cloned.1.call-update
  13.1 0.0 reduce-scatter.4.cloned.1.call-start
  13.2 56.3 %all-reduce.4.cloned.1.call-done = f32[192,256]{1,0:T(8,128)} async-done(((f32[192,256]{1,0:T(8,128)}), f32[192,256]{1,0:T(8,128)}) %all-reduce.4.cloned.1.call-update) | async-done | bytes 196624 | tf_op jit(solution)/shard_map/psum | solution.py:175
  69.5 12.4 %all_gather.7 = f32[768,256]{1,0:T(8,128)S(1)} all-gather(f32[192,256]{1,0:T(8,128)} %all-reduce.4.cloned.1.call-done), channel_id=1, replica_groups=mesh['tok'=4,'row'=8] {'tok'}, dimensions={0}, use_global_device_ids=true | all-gather | bytes 983040 | tf_op jit(solution)/shard_map/all_gather | solution.py:176
  81.9 0.0 all-gather.2.cloned.1.call-done
  81.9 0.0 copy-done.5
  81.9 5.5 fusion
  87.5 0.1 fusion.10
  87.6 0.4 fusion.8
  87.9 17.0 %shard_map.85 = f32[8,256,896]{2,1,0:T(8,128)} custom-call(bf16[256,1024]{1,0:T(8,128)(2,1)S(1)} %get-tuple-element.18.first_ref, bf16[256,1024]{1,0:T(8,128)(2,1)S(1)} %get-tuple-element.24.second_ref, bf16[256,1024]{1,0:T(8,128)(2,1)S(1)} %get-tuple-element.12.third_ref, bf16[1024,7168]{1,0:T(8,128)(2,1)} %weight_ref.5), custom_call_target="tpu_custom_call" | custom-call | flops 11274289152 | bytes 22020096 | tf_op jit(solution)/shard_map/pallas_call | solution.py:84
  104.9 0.0 reduce-scatter.4.cloned.1.call-update
  104.9 0.0 reduce-scatter.6.cloned.1.call-start
  105.0 17.3 %shard_map.86 = f32[8,256,896]{2,1,0:T(8,128)} custom-call(bf16[256,1024]{1,0:T(8,128)(2,1)S(1)} %get-tuple-element.20.first_ref, bf16[256,1024]{1,0:T(8,128)(2,1)S(1)} %get-tuple-element.22.second_ref, bf16[256,1024]{1,0:T(8,128)(2,1)S(1)} %get-tuple-element.14.third_ref, bf16[1024,7168]{1,0:T(8,128)(2,1)} %weight_ref.5), custom_call_target="tpu_custom_call" | custom-call | flops 11274289152 | bytes 22020096 | tf_op jit(solution)/shard_map/pallas_call | solution.py:84
  122.3 0.0 reduce-scatter.6.cloned.1.call-update
  122.4 0.0 reduce-scatter.8.cloned.1.call-start
  122.4 17.1 %shard_map.87 = f32[8,256,896]{2,1,0:T(8,128)} custom-call(bf16[256,1024]{1,0:T(8,128)(2,1)S(1)} %get-tuple-element.19.first_ref, bf16[256,1024]{1,0:T(8,128)(2,1)S(1)} %get-tuple-element.23.second_ref, bf16[256,1024]{1,0:T(8,128)(2,1)S(1)} %get-tuple-element.13.third_ref, bf16[1024,7168]{1,0:T(8,128)(2,1)} %weight_ref.5), custom_call_target="tpu_custom_call" | custom-call | flops 11274289152 | bytes 22020096 | tf_op jit(solution)/shard_map/pallas_call | solution.py:84
  139.5 0.0 reduce-scatter.8.cloned.1.call-update
  139.5 0.2 all-reduce.8.cloned.1.call-start
  139.7 43.1 %reduce-scatter.4.cloned.1.call-done = f32[1,256,896]{2,1,0:T(8,128)} async-done(((f32[8,256,896]{2,1,0:T(8,128)}), f32[1,256,896]{2,1,0:T(8,128)}) %reduce-scatter.4.cloned.1.call-update) | async-done | bytes 917520 | tf_op jit(solution)/shard_map/reduce_scatter | solution.py:186
  182.8 80.5 %reduce-scatter.6.cloned.1.call-done = f32[1,256,896]{2,1,0:T(8,128)} async-done(((f32[8,256,896]{2,1,0:T(8,128)}), f32[1,256,896]{2,1,0:T(8,128)}) %reduce-scatter.6.cloned.1.call-update) | async-done | bytes 917520 | tf_op jit(solution)/shard_map/reduce_scatter | solution.py:186
  263.4 80.3 %reduce-scatter.8.cloned.1.call-done = f32[1,256,896]{2,1,0:T(8,128)} async-done(((f32[8,256,896]{2,1,0:T(8,128)}), f32[1,256,896]{2,1,0:T(8,128)}) %reduce-scatter.8.cloned.1.call-update) | async-done | bytes 917520 | tf_op jit(solution)/shard_map/reduce_scatter | solution.py:186
  343.7 0.0 copy-start.7
  343.7 0.0 copy-start.9
  343.7 0.0 copy-start.11
  343.7 10.4 %fusion.2 = f32[768,768]{1,0:T(8,128)S(1)} fusion(f32[256,896]{1,0:T(8,128)} %bitcast.18, f32[256,896]{1,0:T(8,128)} %bitcast.15, f32[256,896]{1,0:T(8,128)} %bitcast.12), kind=kOutput, calls=%fused_computation.11 | convolution fusion | flops 6343163904 | bytes 5111808 | tf_op jit(solution)/shard_map/dot_general | solution.py:23
  354.2 0.0 copy-done.7
  354.2 0.0 copy-done.9
  354.2 0.0 copy-done.11
  354.2 2.5 fusion.1
  356.7 2.1 pad_maximum_fusion
  358.8 0.0 copy-start.3
  358.8 0.0 all-reduce.8.cloned.1.call-update
  358.9 0.3 all-reduce.6.cloned.1.call-start
  359.1 1.6 copy-done.3
  360.7 9.2 %fusion.12 = f32[768,768]{1,0:T(8,128)} fusion(f32[768,1024]{1,0:T(8,128)S(1)} %copy-done.3), kind=kOutput, calls=%fused_computation.21 | convolution fusion | flops 7247757312 | bytes 5505024 | tf_op jit(solution)/shard_map/dot_general | solution.py:23
  369.9 0.0 all-reduce.6.cloned.1.call-update
  369.9 124.8 %all-reduce.8.cloned.1.call-done = f32[768,1024]{1,0:T(8,128)} async-done(((f32[768,1024]{1,0:T(8,128)}), f32[768,1024]{1,0:T(8,128)}) %all-reduce.8.cloned.1.call-update) | async-done | bytes 3145744 | tf_op jit(solution)/shard_map/psum | solution.py:193
  494.7 3.3 slice.53.square_ref
  498.0 1.2 slice.54.imaged_ref
  499.2 63.7 %all-reduce.6.cloned.1.call-done.gram_ref = f32[768,768]{1,0:T(8,128)} async-done(((f32[768,768]{1,0:T(8,128)}), f32[768,768]{1,0:T(8,128)}) %all-reduce.6.cloned.1.call-update) | async-done | bytes 2359312 | tf_op jit(solution)/shard_map/psum | solution.py:179
  562.9 0.0 copy-start.2
  562.9 1.7 copy-done.2
  564.6 0.0 copy-start.8
  564.6 0.0 copy-start.10
  564.6 0.0 copy-start.12
  564.6 131.1 %shard_map.88 = (f32[768,256]{1,0:T(8,128)S(1)}, f32[768,256]{1,0:T(8,128)S(1)}, f32[256,256]{1,0:T(8,128)}) custom-call(f32[768,768]{1,0:T(8,128)S(1)} %copy-done.2, f32[768,768]{1,0:T(8,128)} %slice.53.square_ref, f32[768,256]{1,0:T(8,128)S(1)} %slice.54.imaged_ref), custom_call_target="tpu_custom_call" | custom-call | tf_op jit(solution)/shard_map/pallas_call | solution.py:153
  695.7 0.0 copy-done.8
  695.7 0.0 copy-done.10
  695.7 0.0 copy-done.12
  695.7 0.0 copy-start.1
  695.7 5.4 convolution_multiply_fusion.1
  701.1 0.0 copy-done.4
  701.1 6.0 convolution_multiply_fusion
  707.1 0.0 copy-done.1
  (1 shorter events, 0.0 us)
Async XLA Ops:
  8.0 1.5 copy-start
  8.0 4.1 copy-start.6
  8.0 73.9 %copy-start.5 = (bf16[256,1024]{1,0:T(8,128)(2,1)S(1)}, bf16[256,1024]{1,0:T(8,128)(2,1)}, u32[]{:S(2)}) copy-start(bf16[256,1024]{1,0:T(8,128)(2,1)} %param.9) | copy-start | bytes 1572868
  8.0 61.5 %all-reduce.4.cloned.1.call-start = ((), (), s32[]{:S(2)}) async-start(), calls=%async_computation.4 | async-start | bytes 393216 | tf_op jit(solution)/shard_map/psum | solution.py:175
  12.1 69.9 %all-gather.2.cloned.1.call-start = ((), (), s32[]{:S(2)}) async-start(), calls=%async_computation.3 | async-start | bytes 3932160 | tf_op jit(solution)/shard_map/all_gather | solution.py:177
  13.1 169.7 %reduce-scatter.4.cloned.1.call-start = ((), (), s32[]{:S(2)}) async-start(), calls=%async_computation.6 | async-start | bytes 8257536 | tf_op jit(solution)/shard_map/reduce_scatter | solution.py:186
  104.9 158.4 %reduce-scatter.6.cloned.1.call-start = ((), (), s32[]{:S(2)}) async-start(), calls=%async_computation.7 | async-start | bytes 8257536 | tf_op jit(solution)/shard_map/reduce_scatter | solution.py:186
  122.4 221.4 %reduce-scatter.8.cloned.1.call-start = ((), (), s32[]{:S(2)}) async-start(), calls=%async_computation.8 | async-start | bytes 8257536 | tf_op jit(solution)/shard_map/reduce_scatter | solution.py:186
  139.5 355.2 %all-reduce.8.cloned.1.call-start = ((), (), s32[]{:S(2)}) async-start(), calls=%async_computation.9 | async-start | bytes 6291456 | tf_op jit(solution)/shard_map/psum | solution.py:193
  343.7 10.5 %copy-start.7 = (f32[1,256,896]{2,1,0:T(8,128)S(1)}, f32[1,256,896]{2,1,0:T(8,128)}, u32[]{:S(2)}) copy-start(f32[1,256,896]{2,1,0:T(8,128)} %reduce-scatter.4.cloned.1.call-done) | copy-start | bytes 2752516
  343.7 10.5 %copy-start.9 = (f32[1,256,896]{2,1,0:T(8,128)S(1)}, f32[1,256,896]{2,1,0:T(8,128)}, u32[]{:S(2)}) copy-start(f32[1,256,896]{2,1,0:T(8,128)} %reduce-scatter.6.cloned.1.call-done) | copy-start | bytes 2752516
  343.7 10.5 %copy-start.11 = (f32[1,256,896]{2,1,0:T(8,128)S(1)}, f32[1,256,896]{2,1,0:T(8,128)}, u32[]{:S(2)}) copy-start(f32[1,256,896]{2,1,0:T(8,128)} %reduce-scatter.8.cloned.1.call-done) | copy-start | bytes 2752516
  358.8 1.9 copy-start.3
  358.9 204.0 %all-reduce.6.cloned.1.call-start = ((), (), s32[]{:S(2)}) async-start(), calls=%async_computation.5 | async-start | bytes 4718592 | tf_op jit(solution)/shard_map/psum | solution.py:179
  562.9 1.7 copy-start.2
  564.6 131.1 %copy-start.8 = (f32[1,256,896]{2,1,0:T(8,128)S(1)}, f32[1,256,896]{2,1,0:T(8,128)}, u32[]{:S(2)}) copy-start(f32[1,256,896]{2,1,0:T(8,128)} %reduce-scatter.4.cloned.1.call-done) | copy-start | bytes 2752516
  564.6 131.1 %copy-start.10 = (f32[1,256,896]{2,1,0:T(8,128)S(1)}, f32[1,256,896]{2,1,0:T(8,128)}, u32[]{:S(2)}) copy-start(f32[1,256,896]{2,1,0:T(8,128)} %reduce-scatter.6.cloned.1.call-done) | copy-start | bytes 2752516
  564.6 131.1 %copy-start.12 = (f32[1,256,896]{2,1,0:T(8,128)S(1)}, f32[1,256,896]{2,1,0:T(8,128)}, u32[]{:S(2)}) copy-start(f32[1,256,896]{2,1,0:T(8,128)} %reduce-scatter.8.cloned.1.call-done) | copy-start | bytes 2752516
  695.7 5.4 copy-start.4
  695.7 11.4 %copy-start.1 = (bf16[3584,256]{1,0:T(8,128)(2,1)S(1)}, bf16[3584,256]{1,0:T(8,128)(2,1)}, u32[]{:S(2)}) copy-start(bf16[3584,256]{1,0:T(8,128)(2,1)} %param.8) | copy-start | bytes 5505028
Sparse Core Ops, SparseCore 0:
  12.2 57.2 all-reduce.3
  105.1 77.7 reduce-scatter.3
  185.3 78.0 reduce-scatter.5
  265.6 78.0 reduce-scatter.7
Sparse Core Ops, SparseCore 1:
  15.0 46.5 all-gather.1
  358.9 135.7 all-reduce.7
  496.9 65.9 all-reduce.5

commit v2 on v1

--- a/solution.py
+++ b/solution.py
@@ -102,15 +102,22 @@
     eye = (
         lax.broadcasted_iota(jnp.int32, (nb, nb), 0) == lax.broadcasted_iota(jnp.int32, (nb, nb), 1)
     ).astype(F32)
-    index = lax.broadcasted_iota(jnp.int32, (nb, 1), 0)
+    index = lax.broadcasted_iota(jnp.int32, (8, 1), 0)
     for at in range(0, size, nb):
         work = jnp.concatenate([table[at : at + nb, at : at + nb], eye], axis=1)
+        groups = [work[k : k + 8, :] for k in range(0, nb, 8)]
         for j in range(nb):
-            scale = lax.rsqrt(work[j : j + 1, j : j + 1])
-            row = work[j : j + 1, :] * scale
-            column = work[:, j : j + 1] * scale
-            work = jnp.where(index == j, row, work - jnp.where(index < j, 0.0, column) * row)
-        small = work[:, nb:]
+            own, place = divmod(j, 8)
+            row = groups[own][place : place + 1, :]
+            inverse = 1.0 / row[:, j : j + 1]
+            for k in range(own, nb // 8):
+                factor = groups[k][:, j : j + 1] * inverse
+                if k == own:
+                    factor = jnp.where(index > place, factor, 0.0)
+                groups[k] = groups[k] - factor * row
+        work = jnp.concatenate(groups, axis=0)
+        pivots = jnp.sum(work[:, :nb] * eye, axis=1, keepdims=True)
+        small = work[:, nb:] * lax.rsqrt(pivots)
         rows = jnp.dot(small, table[at : at + nb, :], precision=HIGH, preferred_element_type=F32)
         table[at : at + nb, :] = rows
         if at + nb < size:
@@ -172,11 +179,11 @@
     width = up_weight.shape[1] // blocks
     own = lax.axis_index("row")
 
-    code = lax.psum(jnp.dot(hidden, down_in, preferred_element_type=F32), "row")
-    code = lax.all_gather(code, "tok", axis=0, tiled=True)
+    code = lax.all_gather(jnp.dot(hidden, down_in, preferred_element_type=F32), "row")
+    code = lax.all_gather(jnp.sum(code, axis=0), "tok", axis=0, tiled=True)
     base = lax.all_gather(resid.astype(F32), "tok", axis=0, tiled=True)
     acts = base + jnp.dot(code, down_out.astype(F32), precision=HIGH)
-    gram = lax.psum(outer(acts, acts), "row")
+    gram = outer(acts, acts) / lax.axis_size("tok")
 
     parts = split_rows(acts)
     chunk = 256 if tokens % 256 == 0 else tokens
@@ -188,10 +195,10 @@
 
     begin = lax.dynamic_slice_in_dim(start, own * width, width, axis=0).astype(F32)
     sums = jnp.concatenate(
-        [outer(applied, applied), jnp.dot(applied, begin, precision=HIGH)], axis=1
+        [gram, outer(applied, applied), jnp.dot(applied, begin, precision=HIGH)], axis=1
     )
     sums = lax.psum(sums, ("tok", "row"))
-    square, imaged = sums[:, :tokens], sums[:, tokens:]
+    gram, square, imaged = sums[:, :tokens], sums[:, tokens : 2 * tokens], sums[:, 2 * tokens :]
 
     left_coef, right_coef, core = coefficients(gram, square, imaged)
     left = inner(acts, left_coef)

time: 722 us -> 675 us (0.935)
  waiting for transfers between devices: 449 us -> 399 us
    psum x2 -> x0, waiting for transfers between devices: 120 us -> none  [the longest x1 63.7 us: token_space(): gram = lax.psum(outer(acts, acts), 'row')]
    all_gather x1, waiting for transfers between devices: 0.01 us -> 29.3 us  [token_space(): base = lax.all_gather(resid.astype(F32), 'tok', axis=0, tiled=True)]
    all_gather x0 -> x1, waiting for transfers between devices: none -> 26.8 us  [token_space(): lax.all_gather(jnp.dot(hidden, down_in, preferred_element_type=F32), 'row')]
    psum x1, waiting for transfers between devices: 125 us -> 148 us  [token_space(): sums = lax.psum(sums, ('tok', 'row'))]
    reduce_scatter x3, waiting for transfers between devices: 204 us -> 195 us  [token_space(): lax.psum_scatter(block, 'row', scatter_dimension=0, tiled=True)[0]]
  transfers between devices with their start and end apart: 7 -> 6, of which waited for: 6 -> 6; matrix products, arithmetic and copies ran while one was open for 2% -> 2% of each run, Pallas kernels for 5% -> 5%
where the time goes in v2:
time: 675 us; the launch traced here: 667 us
  waiting for transfers between devices  399 us (59%)
  Pallas kernels  182 us (27%)
  matrix products  41.9 us (6%)
  blocking collectives  15.1 us (2%)
  between operations  14.7 us (2%)
  local copies, waits for them, and re-layouts  8.93 us (1%)
    reduce_scatter x3, waiting for transfers between devices, token_space(): lax.psum_scatter(block, 'row', scatter_dimension=0, tiled=True)[0]  195 us
    psum x1, waiting for transfers between devices, token_space(): sums = lax.psum(sums, ('tok', 'row'))  148 us
    pallas_call x1, Pallas kernels, coefficients(): pl.pallas_call(coefficient_kernel, in_specs=[pl.BlockSpec(memory_space=pl...  130 us
    pallas_call x3, Pallas kernels, applied_blocks(): pl.pallas_call(product_kernel, grid=(blocks,), in_specs=[whole, whole, wh...  51.5 us
    all_gather x1, waiting for transfers between devices, token_space(): base = lax.all_gather(resid.astype(F32), 'tok', axis=0, tiled=True)  29.3 us
    all_gather x1, waiting for transfers between devices, token_space(): lax.all_gather(jnp.dot(hidden, down_in, preferred_element_type=F32), 'row')  26.8 us
    dot_general x2, matrix products, outer(): lax.dot_general(first, second, (((1,), (1,)), ((), ())), precision=HIGH,...  19.7 us
    all_gather x1, blocking collectives, token_space(): code = lax.all_gather(jnp.sum(code, axis=0), 'tok', axis=0, tiled=True)  15.1 us
  transfers between devices with their start and end apart: 6, of which 6 were waited for; matrix products, arithmetic and copies ran while one was open for 2% of the time, Pallas kernels for 5%

profile of v2, /device:TPU:0, one launch (start us, length us, event | category | flops | bytes accessed | tf_op | source)
XLA Modules:
  0.0 667.4 jit_solution(9982632934775306317)
XLA Ops:
  7.2 0.0 copy-start
  7.2 0.0 copy-start.6
  7.2 0.0 all-gather.6.cloned.1.call-start
  7.2 1.4 copy-done
  8.7 2.5 fusion.12
  11.2 0.0 copy-start.5
  11.2 0.0 all-gather.6.cloned.1.call-update
  11.2 0.0 all-gather.4.cloned.1.call-start
  11.3 0.0 copy-done.6
  11.3 1.0 convert_element_type.14
  12.3 0.0 all-gather.4.cloned.1.call-update
  12.3 0.0 reduce-scatter.4.cloned.1.call-start
  12.3 26.8 %all-gather.6.cloned.1.call-done = f32[1536,256]{1,0:T(8,128)} async-done(((f32[192,256]{1,0:T(8,128)}), f32[1536,256]{1,0:T(8,128)}) %all-gather.6.cloned.1.call-update) | async-done | bytes 1572880 | tf_op jit(solution)/shard_map/all_gather | solution.py:182
  39.2 1.5 reduce_sum.9
  40.7 15.1 %all_gather.15 = f32[768,256]{1,0:T(8,128)S(1)} all-gather(f32[192,256]{1,0:T(8,128)S(1)} %reduce_sum.9), channel_id=1, replica_groups=mesh['tok'=4,'row'=8] {'tok'}, dimensions={0}, use_global_device_ids=true | all-gather | bytes 983040 | tf_op jit(solution)/shard_map/all_gather | solution.py:183
  55.8 29.3 %all-gather.4.cloned.1.call-done = f32[768,1024]{1,0:T(8,128)} async-done(((f32[192,1024]{1,0:T(8,128)}), f32[768,1024]{1,0:T(8,128)}) %all-gather.4.cloned.1.call-update) | async-done | bytes 3145744 | tf_op jit(solution)/shard_map/all_gather | solution.py:184
  85.1 0.0 copy-done.5
  85.1 5.5 fusion
  90.6 0.1 fusion.11
  90.8 0.4 fusion.9
  91.1 17.0 %shard_map.85 = f32[8,256,896]{2,1,0:T(8,128)} custom-call(bf16[256,1024]{1,0:T(8,128)(2,1)S(1)} %get-tuple-element.20.first_ref, bf16[256,1024]{1,0:T(8,128)(2,1)S(1)} %get-tuple-element.26.second_ref, bf16[256,1024]{1,0:T(8,128)(2,1)S(1)} %get-tuple-element.14.third_ref, bf16[1024,7168]{1,0:T(8,128)(2,1)} %weight_ref.5), custom_call_target="tpu_custom_call" | custom-call | flops 11274289152 | bytes 22020096 | tf_op jit(solution)/shard_map/pallas_call | solution.py:84
  108.1 0.0 reduce-scatter.4.cloned.1.call-update
  108.1 0.0 reduce-scatter.6.cloned.1.call-start
  108.2 17.4 %shard_map.86 = f32[8,256,896]{2,1,0:T(8,128)} custom-call(bf16[256,1024]{1,0:T(8,128)(2,1)S(1)} %get-tuple-element.22.first_ref, bf16[256,1024]{1,0:T(8,128)(2,1)S(1)} %get-tuple-element.24.second_ref, bf16[256,1024]{1,0:T(8,128)(2,1)S(1)} %get-tuple-element.16.third_ref, bf16[1024,7168]{1,0:T(8,128)(2,1)} %weight_ref.5), custom_call_target="tpu_custom_call" | custom-call | flops 11274289152 | bytes 22020096 | tf_op jit(solution)/shard_map/pallas_call | solution.py:84
  125.6 0.0 reduce-scatter.6.cloned.1.call-update
  125.6 0.0 reduce-scatter.8.cloned.1.call-start
  125.6 17.1 %shard_map.87 = f32[8,256,896]{2,1,0:T(8,128)} custom-call(bf16[256,1024]{1,0:T(8,128)(2,1)S(1)} %get-tuple-element.21.first_ref, bf16[256,1024]{1,0:T(8,128)(2,1)S(1)} %get-tuple-element.25.second_ref, bf16[256,1024]{1,0:T(8,128)(2,1)S(1)} %get-tuple-element.15.third_ref, bf16[1024,7168]{1,0:T(8,128)(2,1)} %weight_ref.5), custom_call_target="tpu_custom_call" | custom-call | flops 11274289152 | bytes 22020096 | tf_op jit(solution)/shard_map/pallas_call | solution.py:84
  142.8 0.0 copy-start.2
  142.8 0.0 reduce-scatter.8.cloned.1.call-update
  142.8 0.2 all-reduce.2.cloned.1.call-start
  143.0 1.7 copy-done.2
  144.7 9.2 %convolution_multiply_fusion = f32[768,768]{1,0:T(8,128)} fusion(f32[768,1024]{1,0:T(8,128)S(1)} %copy-done.2), kind=kOutput, calls=%fused_computation.8 | convolution fusion | flops 7248347136 | bytes 5505024 | tf_op jit(solution)/shard_map/dot_general | solution.py:23
  153.9 34.0 %reduce-scatter.4.cloned.1.call-done = f32[1,256,896]{2,1,0:T(8,128)} async-done(((f32[8,256,896]{2,1,0:T(8,128)}), f32[1,256,896]{2,1,0:T(8,128)}) %reduce-scatter.4.cloned.1.call-update) | async-done | bytes 917520 | tf_op jit(solution)/shard_map/reduce_scatter | solution.py:193
  188.0 80.3 %reduce-scatter.6.cloned.1.call-done = f32[1,256,896]{2,1,0:T(8,128)} async-done(((f32[8,256,896]{2,1,0:T(8,128)}), f32[1,256,896]{2,1,0:T(8,128)}) %reduce-scatter.6.cloned.1.call-update) | async-done | bytes 917520 | tf_op jit(solution)/shard_map/reduce_scatter | solution.py:193
  268.3 80.2 %reduce-scatter.8.cloned.1.call-done = f32[1,256,896]{2,1,0:T(8,128)} async-done(((f32[8,256,896]{2,1,0:T(8,128)}), f32[1,256,896]{2,1,0:T(8,128)}) %reduce-scatter.8.cloned.1.call-update) | async-done | bytes 917520 | tf_op jit(solution)/shard_map/reduce_scatter | solution.py:193
  348.5 0.0 copy-start.7
  348.5 0.0 copy-start.8
  348.5 0.0 copy-start.10
  348.5 10.5 %fusion.2 = f32[768,768]{1,0:T(8,128)S(1)} fusion(f32[256,896]{1,0:T(8,128)} %bitcast.20, f32[256,896]{1,0:T(8,128)} %bitcast.17, f32[256,896]{1,0:T(8,128)} %bitcast.14), kind=kOutput, calls=%fused_computation.12 | convolution fusion | flops 6343163904 | bytes 5111808 | tf_op jit(solution)/shard_map/dot_general | solution.py:23
  359.0 0.0 copy-done.7
  359.0 0.0 copy-done.8
  359.0 0.0 copy-done.10
  359.0 0.0 copy-start.4
  359.0 2.7 fusion.1
  361.7 0.0 copy-done.4
  361.7 2.8 pad_maximum_fusion
  364.5 0.0 all-reduce.2.cloned.1.call-update
  364.6 148.3 %all-reduce.2.cloned.1.call-done = f32[768,1792]{1,0:T(8,128)} async-done(((f32[768,1792]{1,0:T(8,128)}), f32[768,1792]{1,0:T(8,128)}) %all-reduce.2.cloned.1.call-update) | async-done | bytes 5505040 | tf_op jit(solution)/shard_map/psum | solution.py:200
  512.9 4.1 fusion.8
  517.0 1.2 slice.59.imaged_ref
  518.2 0.0 copy-start.9
  518.2 0.0 copy-start.11
  518.2 130.4 %shard_map.88 = (f32[768,256]{1,0:T(8,128)S(1)}, f32[768,256]{1,0:T(8,128)S(1)}, f32[256,256]{1,0:T(8,128)}) custom-call(f32[768,768]{1,0:T(8,128)S(1)} %get-tuple-element.10.gram_ref, f32[768,768]{1,0:T(8,128)} %get-tuple-element.9.square_ref, f32[768,256]{1,0:T(8,128)S(1)} %slice.59.imaged_ref), custom_call_target="tpu_custom_call" | custom-call | tf_op jit(solution)/shard_map/pallas_call | solution.py:160
  648.6 0.0 copy-start.3
  648.6 0.0 copy-done.9
  648.6 0.0 copy-done.11
  648.6 0.0 copy-start.1
  648.6 5.4 convolution_multiply_fusion.2
  654.0 0.0 copy-done.3
  654.0 6.0 convolution_multiply_fusion.1
  660.0 0.0 copy-done.1
Async XLA Ops:
  7.2 1.5 copy-start
  7.2 4.1 copy-start.6
  7.2 32.0 %all-gather.6.cloned.1.call-start = ((), (), s32[]{:S(2)}) async-start(), calls=%async_computation.8 | async-start | bytes 1769472 | tf_op jit(solution)/shard_map/all_gather | solution.py:182
  11.2 73.9 %copy-start.5 = (bf16[256,1024]{1,0:T(8,128)(2,1)S(1)}, bf16[256,1024]{1,0:T(8,128)(2,1)}, u32[]{:S(2)}) copy-start(bf16[256,1024]{1,0:T(8,128)(2,1)} %param.9) | copy-start | bytes 1572868
  11.2 73.9 %all-gather.4.cloned.1.call-start = ((), (), s32[]{:S(2)}) async-start(), calls=%async_computation.3 | async-start | bytes 3932160 | tf_op jit(solution)/shard_map/all_gather | solution.py:184
  12.3 175.7 %reduce-scatter.4.cloned.1.call-start = ((), (), s32[]{:S(2)}) async-start(), calls=%async_computation.4 | async-start | bytes 8257536 | tf_op jit(solution)/shard_map/reduce_scatter | solution.py:193
  108.1 160.1 %reduce-scatter.6.cloned.1.call-start = ((), (), s32[]{:S(2)}) async-start(), calls=%async_computation.5 | async-start | bytes 8257536 | tf_op jit(solution)/shard_map/reduce_scatter | solution.py:193
  125.6 222.9 %reduce-scatter.8.cloned.1.call-start = ((), (), s32[]{:S(2)}) async-start(), calls=%async_computation.6 | async-start | bytes 8257536 | tf_op jit(solution)/shard_map/reduce_scatter | solution.py:193
  142.8 2.0 copy-start.2
  142.8 370.1 %all-reduce.2.cloned.1.call-start = ((), (), s32[]{:S(2)}) async-start(), calls=%async_computation.7 | async-start | bytes 11010048 | tf_op jit(solution)/shard_map/psum | solution.py:200
  348.5 10.5 %copy-start.7 = (f32[1,256,896]{2,1,0:T(8,128)S(1)}, f32[1,256,896]{2,1,0:T(8,128)}, u32[]{:S(2)}) copy-start(f32[1,256,896]{2,1,0:T(8,128)} %reduce-scatter.4.cloned.1.call-done) | copy-start | bytes 2752516
  348.5 10.5 %copy-start.8 = (f32[1,256,896]{2,1,0:T(8,128)S(1)}, f32[1,256,896]{2,1,0:T(8,128)}, u32[]{:S(2)}) copy-start(f32[1,256,896]{2,1,0:T(8,128)} %reduce-scatter.6.cloned.1.call-done) | copy-start | bytes 2752516
  348.5 10.5 %copy-start.10 = (f32[1,256,896]{2,1,0:T(8,128)S(1)}, f32[1,256,896]{2,1,0:T(8,128)}, u32[]{:S(2)}) copy-start(f32[1,256,896]{2,1,0:T(8,128)} %reduce-scatter.8.cloned.1.call-done) | copy-start | bytes 2752516
  359.0 2.7 copy-start.4
  518.2 130.4 %copy-start.9 = (f32[1,256,896]{2,1,0:T(8,128)S(1)}, f32[1,256,896]{2,1,0:T(8,128)}, u32[]{:S(2)}) copy-start(f32[1,256,896]{2,1,0:T(8,128)} %reduce-scatter.6.cloned.1.call-done) | copy-start | bytes 2752516
  518.2 130.4 %copy-start.11 = (f32[1,256,896]{2,1,0:T(8,128)S(1)}, f32[1,256,896]{2,1,0:T(8,128)}, u32[]{:S(2)}) copy-start(f32[1,256,896]{2,1,0:T(8,128)} %reduce-scatter.8.cloned.1.call-done) | copy-start | bytes 2752516
  648.6 5.4 copy-start.3
  648.6 11.4 %copy-start.1 = (bf16[3584,256]{1,0:T(8,128)(2,1)S(1)}, bf16[3584,256]{1,0:T(8,128)(2,1)}, u32[]{:S(2)}) copy-start(bf16[3584,256]{1,0:T(8,128)(2,1)} %param.8) | copy-start | bytes 5505028
Sparse Core Ops, SparseCore 0:
  11.4 27.7 all-gather.5
  41.6 43.4 all-gather.3
  108.2 79.6 reduce-scatter.3
  190.1 78.0 reduce-scatter.5
  270.4 78.0 reduce-scatter.7
  364.7 148.1 all-reduce.1
